TPU v7x, 32 devices: a whole 2x2x4 slice. The times are simulated.
32 devices in a mesh: dp: 8 (over y, x, core), mp: 4 (over z).
Axes of the slice: x: 2, y: 2, z: 4, core: 2. Of those that a mesh axis runs over, the one named last changes fastest.
Arguments:
- activations: bfloat16 [128, 288, 768], P(('dp', 'mp')), may hold values from -2.5 to 2.5
- cotangent: bfloat16 [128, 288, 768], P(('dp', 'mp')), may hold values from -2.5 to 2.5
- segments: int32 [128, 288], P('dp'), may hold values from 0 to 2, never falling along the last dimension, each value on 1 to 160 neighbouring positions
- triple_weight: bfloat16 [3, 768, 768], P(None, None, 'mp'), may hold values from -0.21875 to 0.21875
- query_value_bias: bfloat16 [2, 12, 64], P(None, 'mp'), may hold values from -1.5 to 1.5
- output_weight: bfloat16 [768, 768], P('mp'), may hold values from -0.875 to 0.875
- expand_weight: bfloat16 [768, 3072], P(None, 'mp'), may hold values from -0.21875 to 0.21875
- expand_bias: bfloat16 [48, 64], P('mp'), may hold values from -1.5 to 1.5
- shrink_weight: bfloat16 [3072, 768], P('mp'), may hold values from -0.109375 to 0.109375
- vector_params: bfloat16 [6, 768], replicated
- triple_master: float32 [3, 768, 768], P(None, 'dp', 'mp'), may hold values from -0.21875 to 0.21875
- triple_first: float32 [3, 768, 768], P(None, 'dp', 'mp'), may hold values from -144 to 144
- triple_second: float32 [3, 768, 768], P(None, 'dp', 'mp'), may hold values from 2211.84 to 8847.36
- query_value_master: float32 [2, 12, 64], P(None, 'mp', 'dp'), may hold values from -1.5 to 1.5
- query_value_first: float32 [2, 12, 64], P(None, 'mp', 'dp'), may hold values from -192 to 192
- query_value_second: float32 [2, 12, 64], P(None, 'mp', 'dp'), may hold values from 3944.448 to 15851.52
- output_master: float32 [768, 768], P('mp', 'dp'), may hold values from -0.875 to 0.875
- output_first: float32 [768, 768], P('mp', 'dp'), may hold values from -57.6 to 57.6
- output_second: float32 [768, 768], P('mp', 'dp'), may hold values from 353.8944 to 1400.832
- expand_master: float32 [768, 3072], P('dp', 'mp'), may hold values from -0.21875 to 0.21875
- expand_first: float32 [768, 3072], P('dp', 'mp'), may hold values from -96 to 96
- expand_second: float32 [768, 3072], P('dp', 'mp'), may hold values from 995.328 to 3944.448
- expand_bias_master: float32 [48, 64], P('mp', 'dp'), may hold values from -1.5 to 1.5
- expand_bias_first: float32 [48, 64], P('mp', 'dp'), may hold values from -96 to 96
- expand_bias_second: float32 [48, 64], P('mp', 'dp'), may hold values from 995.328 to 3944.448
- shrink_master: float32 [3072, 768], P('mp', 'dp'), may hold values from -0.109375 to 0.109375
- shrink_first: float32 [3072, 768], P('mp', 'dp'), may hold values from -192 to 192
- shrink_second: float32 [3072, 768], P('mp', 'dp'), may hold values from 3944.448 to 15851.52
- vector_master: float32 [6, 768], P(None, ('dp', 'mp'))
- vector_first: float32 [6, 768], P(None, ('dp', 'mp')), may hold values from -384 to 384
- vector_second: float32 [6, 768], P(None, ('dp', 'mp')), may hold values from 15851.52 to 62668.8
Outputs:
- block_output: bfloat16 [128, 288, 768], P(('dp', 'mp'))
- input_grad: float32 [128, 288, 768], P(('dp', 'mp'))
- triple_master_new: float32 [3, 768, 768], P(None, 'dp', 'mp')
- triple_first_new: float32 [3, 768, 768], P(None, 'dp', 'mp')
- triple_second_new: float32 [3, 768, 768], P(None, 'dp', 'mp')
- triple_copy: bfloat16 [3, 768, 768], P(None, 'dp', 'mp')
- query_value_master_new: float32 [2, 12, 64], P(None, 'mp', 'dp')
- query_value_first_new: float32 [2, 12, 64], P(None, 'mp', 'dp')
- query_value_second_new: float32 [2, 12, 64], P(None, 'mp', 'dp')
- query_value_copy: bfloat16 [2, 12, 64], P(None, 'mp', 'dp')
- output_master_new: float32 [768, 768], P('mp', 'dp')
- output_first_new: float32 [768, 768], P('mp', 'dp')
- output_second_new: float32 [768, 768], P('mp', 'dp')
- output_copy: bfloat16 [768, 768], P('mp', 'dp')
- expand_master_new: float32 [768, 3072], P('dp', 'mp')
- expand_first_new: float32 [768, 3072], P('dp', 'mp')
- expand_second_new: float32 [768, 3072], P('dp', 'mp')
- expand_copy: bfloat16 [768, 3072], P('dp', 'mp')
- expand_bias_master_new: float32 [48, 64], P('mp', 'dp')
- expand_bias_first_new: float32 [48, 64], P('mp', 'dp')
- expand_bias_second_new: float32 [48, 64], P('mp', 'dp')
- expand_bias_copy: bfloat16 [48, 64], P('mp', 'dp')
- shrink_master_new: float32 [3072, 768], P('mp', 'dp')
- shrink_first_new: float32 [3072, 768], P('mp', 'dp')
- shrink_second_new: float32 [3072, 768], P('mp', 'dp')
- shrink_copy: bfloat16 [3072, 768], P('mp', 'dp')
- vector_master_new: float32 [6, 768], P(None, ('dp', 'mp'))
- vector_first_new: float32 [6, 768], P(None, ('dp', 'mp'))
- vector_second_new: float32 [6, 768], P(None, ('dp', 'mp'))
- vector_copy: bfloat16 [6, 768], P(None, ('dp', 'mp'))
Inputs may be any that keep to these rules, and one draw needn't show every extreme that they name: `segments`: along a row the pair numbers never fall; each pair has 1 to 160 tokens, and each row has one pair of exactly 160.
All inputs are finite; a program needn't handle non-finite values.
Results may differ from a plain program's by a relative error of at most 0.018.
Values may be sent and summed in bfloat16 or wider, within the bound.
A program may use at most 256 MiB of HBM per device.

v0:
```python
import jax
import jax.numpy as jnp
from jax import lax
from jax.sharding import PartitionSpec as P

D = 768
HEAD = 64
FF = 3072
MB = 4
STEP = 10
NORM_EPS = 1e-05
BETA_ONE = 0.5
BETA_TWO = 0.6
ADAM_EPS = 1e-08
WEIGHT_DECAY = 0.01
MASKED = -1e30
SQRT_HALF = 0.7071067811865476
INV_ROOT_TAU = 0.3989422804014327


def norm_forward(summed, gain, shift):
    centre = summed - jnp.mean(summed, axis=-1, keepdims=True)
    scale = lax.rsqrt(jnp.mean(centre * centre, axis=-1, keepdims=True) + NORM_EPS)
    normed = centre * scale
    return (gain * normed + shift, normed, scale)


def norm_backward(gradient, gain, normed, scale):
    scaled = gradient * gain
    centred = scaled - jnp.mean(scaled, axis=-1, keepdims=True)
    return scale * (centred - normed * jnp.mean(scaled * normed, axis=-1, keepdims=True))


def gelu(inputs):
    return 0.5 * inputs * (1.0 + jax.scipy.special.erf(inputs * SQRT_HALF))


def gelu_slope(inputs):
    cumulative = 0.5 * (1.0 + jax.scipy.special.erf(inputs * SQRT_HALF))
    return cumulative + inputs * jnp.exp(-0.5 * inputs * inputs) * INV_ROOT_TAU


def attention_scores(projected, allowed, head_count):
    row_count, length = (projected.shape[0], projected.shape[1])
    parted = projected.reshape(row_count, length, 3, head_count, HEAD)
    queries = parted[:, :, 0]
    key_rows = parted[:, :, 1]
    values = parted[:, :, 2]
    scores = jnp.einsum(
        "rqhc,rkhc->rhqk", queries, key_rows, preferred_element_type=jnp.float32
    ) * HEAD ** (-0.5)
    return (jnp.where(allowed[:, None], scores, MASKED), queries, key_rows, values)


def attend(projected, allowed, head_count):
    row_count, length = (projected.shape[0], projected.shape[1])
    scores, queries, key_rows, values = attention_scores(projected, allowed, head_count)
    row_max = jnp.max(scores, axis=-1, keepdims=True)
    weights = jnp.exp(scores - row_max)
    row_total = jnp.sum(weights, axis=-1, keepdims=True)
    probabilities = (weights / row_total).astype(jnp.bfloat16)
    context = jnp.einsum(
        "rhqk,rkhc->rqhc", probabilities, values, preferred_element_type=jnp.float32
    )
    context = context.astype(jnp.bfloat16).reshape(row_count, length, head_count * HEAD)
    return (context, row_max + jnp.log(row_total))


def attend_back(projected, allowed, log_total, dcontext, head_count):
    row_count, length = (projected.shape[0], projected.shape[1])
    scores, queries, key_rows, values = attention_scores(projected, allowed, head_count)
    probabilities = jnp.exp(scores - log_total)
    grad_context = dcontext.reshape(row_count, length, head_count, HEAD)
    grad_values = jnp.einsum(
        "rhqk,rqhc->rkhc",
        probabilities.astype(jnp.bfloat16),
        grad_context,
        preferred_element_type=jnp.float32,
    )
    grad_probs = jnp.einsum(
        "rqhc,rkhc->rhqk", grad_context, values, preferred_element_type=jnp.float32
    )
    row_inner = jnp.sum(probabilities * grad_probs, axis=-1, keepdims=True)
    grad_scores = (probabilities * (grad_probs - row_inner)).astype(jnp.bfloat16)
    grad_queries = jnp.einsum(
        "rhqk,rkhc->rqhc", grad_scores, key_rows, preferred_element_type=jnp.float32
    ) * HEAD ** (-0.5)
    grad_keys = jnp.einsum(
        "rhqk,rqhc->rkhc", grad_scores, queries, preferred_element_type=jnp.float32
    ) * HEAD ** (-0.5)
    stacked = jnp.stack([grad_queries, grad_keys, grad_values], axis=2)
    return stacked.astype(jnp.bfloat16).reshape(row_count, length, 3, head_count * HEAD)


def adam_update(master, first, second, gradient, rate):
    first_new = BETA_ONE * first + (1.0 - BETA_ONE) * gradient
    second_new = BETA_TWO * second + (1.0 - BETA_TWO) * gradient * gradient
    corrected = first_new / (1.0 - BETA_ONE**STEP)
    spread = jnp.sqrt(second_new / (1.0 - BETA_TWO**STEP))
    master_new = master - rate * (corrected / (spread + ADAM_EPS) + WEIGHT_DECAY * master)
    return (master_new, first_new, second_new, master_new.astype(jnp.bfloat16))


def per_device(
    activations,
    cotangent,
    segments,
    triple_weight,
    query_value_bias,
    output_weight,
    expand_weight,
    expand_bias,
    shrink_weight,
    vector_params,
    triple_master,
    triple_first,
    triple_second,
    query_value_master,
    query_value_first,
    query_value_second,
    output_master,
    output_first,
    output_second,
    expand_master,
    expand_first,
    expand_second,
    expand_bias_master,
    expand_bias_first,
    expand_bias_second,
    shrink_master,
    shrink_first,
    shrink_second,
    vector_master,
    vector_first,
    vector_second,
):
    group_count = lax.axis_size("mp")
    triple_local, query_value_local, output_local = (triple_weight, query_value_bias, output_weight)
    expand_local, expand_bias_local, shrink_local = (expand_weight, expand_bias, shrink_weight)
    gains = vector_params.astype(jnp.float32)
    head_count = triple_local.shape[2] // HEAD
    width = head_count * HEAD
    bias_pair = query_value_local.reshape(2, width).astype(jnp.float32)
    bias_add = jnp.stack([bias_pair[0], jnp.zeros_like(bias_pair[0]), bias_pair[1]])
    expand_shift = expand_bias_local.reshape(-1).astype(jnp.float32)
    micro_rows = activations.shape[0] // MB
    length = activations.shape[1]
    segment_blocks = segments.reshape(group_count, MB, micro_rows, length)
    triple_grad = jnp.zeros(triple_local.shape, jnp.float32)
    bias_grad = jnp.zeros((3, width), jnp.float32)
    output_grad = jnp.zeros(output_local.shape, jnp.float32)
    expand_grad = jnp.zeros(expand_local.shape, jnp.float32)
    expand_shift_grad = jnp.zeros(expand_shift.shape, jnp.float32)
    shrink_grad = jnp.zeros(shrink_local.shape, jnp.float32)
    vector_grad = jnp.zeros(gains.shape, jnp.float32)
    outputs = []
    input_grads = []
    for micro_index in range(MB):
        own_inputs = activations[micro_index * micro_rows : (micro_index + 1) * micro_rows]
        own_back = cotangent[micro_index * micro_rows : (micro_index + 1) * micro_rows].astype(
            jnp.float32
        )
        full_inputs = lax.all_gather(own_inputs, "mp", axis=0, tiled=True)
        seg_rows = segment_blocks[:, micro_index].reshape(-1, length)
        allowed = seg_rows[:, :, None] == seg_rows[:, None, :]
        projected = jnp.einsum(
            "rld,jde->rlje", full_inputs, triple_local, preferred_element_type=jnp.float32
        )
        projected = (projected + bias_add).astype(jnp.bfloat16)
        context, log_total = attend(projected, allowed, head_count)
        attended = lax.psum_scatter(
            jnp.einsum(
                "rle,ed->rld", context, output_local, preferred_element_type=jnp.float32
            ).astype(jnp.bfloat16),
            "mp",
            scatter_dimension=0,
            tiled=True,
        ).astype(jnp.float32)
        mixed = own_inputs.astype(jnp.float32) + attended + gains[2]
        hidden, normed_one, scale_one = norm_forward(mixed, gains[0], gains[1])
        hidden_low = hidden.astype(jnp.bfloat16)
        full_hidden = lax.all_gather(hidden_low, "mp", axis=0, tiled=True)
        expanded = (
            jnp.einsum("rld,df->rlf", full_hidden, expand_local, preferred_element_type=jnp.float32)
            + expand_shift
        )
        active = gelu(expanded).astype(jnp.bfloat16)
        shrunk = lax.psum_scatter(
            jnp.einsum(
                "rlf,fd->rld", active, shrink_local, preferred_element_type=jnp.float32
            ).astype(jnp.bfloat16),
            "mp",
            scatter_dimension=0,
            tiled=True,
        ).astype(jnp.float32)
        summed = hidden + shrunk + gains[5]
        result, normed_two, scale_two = norm_forward(summed, gains[3], gains[4])
        outputs.append(result.astype(jnp.bfloat16))
        dsummed = norm_backward(own_back, gains[3], normed_two, scale_two)
        dsummed_low = dsummed.astype(jnp.bfloat16)
        full_dsummed = lax.all_gather(dsummed_low, "mp", axis=0, tiled=True)
        dactive = jnp.einsum(
            "rld,fd->rlf", full_dsummed, shrink_local, preferred_element_type=jnp.float32
        )
        dexpanded = (dactive * gelu_slope(expanded)).astype(jnp.bfloat16)
        dhidden_part = lax.psum_scatter(
            jnp.einsum(
                "rlf,df->rld", dexpanded, expand_local, preferred_element_type=jnp.float32
            ).astype(jnp.bfloat16),
            "mp",
            scatter_dimension=0,
            tiled=True,
        ).astype(jnp.float32)
        dhidden = dsummed + dhidden_part
        dmixed = norm_backward(dhidden, gains[0], normed_one, scale_one)
        dmixed_low = dmixed.astype(jnp.bfloat16)
        full_dmixed = lax.all_gather(dmixed_low, "mp", axis=0, tiled=True)
        dcontext = jnp.einsum(
            "rld,ed->rle", full_dmixed, output_local, preferred_element_type=jnp.float32
        ).astype(jnp.bfloat16)
        dprojected = attend_back(projected, allowed, log_total, dcontext, head_count)
        dinput_part = lax.psum_scatter(
            jnp.einsum(
                "rlje,jde->rld", dprojected, triple_local, preferred_element_type=jnp.float32
            ).astype(jnp.bfloat16),
            "mp",
            scatter_dimension=0,
            tiled=True,
        ).astype(jnp.float32)
        input_grads.append(dmixed + dinput_part)
        triple_grad = triple_grad + jnp.einsum(
            "rld,rlje->jde", full_inputs, dprojected, preferred_element_type=jnp.float32
        )
        bias_grad = bias_grad + jnp.sum(dprojected, axis=(0, 1), dtype=jnp.float32)
        output_grad = output_grad + jnp.einsum(
            "rle,rld->ed", context, full_dmixed, preferred_element_type=jnp.float32
        )
        expand_grad = expand_grad + jnp.einsum(
            "rld,rlf->df", full_hidden, dexpanded, preferred_element_type=jnp.float32
        )
        expand_shift_grad = expand_shift_grad + jnp.sum(dexpanded, axis=(0, 1), dtype=jnp.float32)
        shrink_grad = shrink_grad + jnp.einsum(
            "rlf,rld->fd", active, full_dsummed, preferred_element_type=jnp.float32
        )
        vector_grad = vector_grad + jnp.stack(
            [
                jnp.sum(dhidden * normed_one, axis=(0, 1)),
                jnp.sum(dhidden, axis=(0, 1)),
                jnp.sum(dmixed, axis=(0, 1)),
                jnp.sum(own_back * normed_two, axis=(0, 1)),
                jnp.sum(own_back, axis=(0, 1)),
                jnp.sum(dsummed, axis=(0, 1)),
            ]
        )
    query_value_grad = jnp.stack([bias_grad[0], bias_grad[2]]).reshape(2, head_count, HEAD)
    expand_bias_grad = expand_shift_grad.reshape(-1, HEAD)
    gradients = (
        triple_grad,
        query_value_grad,
        output_grad,
        expand_grad,
        expand_bias_grad,
        shrink_grad,
    )
    gradients = (
        lax.psum_scatter(gradients[0], "dp", scatter_dimension=1, tiled=True),
        lax.psum_scatter(gradients[1], "dp", scatter_dimension=2, tiled=True),
        lax.psum_scatter(gradients[2], "dp", scatter_dimension=1, tiled=True),
        lax.psum_scatter(gradients[3], "dp", scatter_dimension=0, tiled=True),
        lax.psum_scatter(gradients[4], "dp", scatter_dimension=1, tiled=True),
        lax.psum_scatter(gradients[5], "dp", scatter_dimension=1, tiled=True),
    )
    vector_reduced = lax.psum_scatter(vector_grad, ("dp", "mp"), scatter_dimension=1, tiled=True)
    triple_out = adam_update(triple_master, triple_first, triple_second, gradients[0], D ** (-0.5))
    query_value_out = adam_update(
        query_value_master, query_value_first, query_value_second, gradients[1], 0.5
    )
    output_out = adam_update(
        output_master, output_first, output_second, gradients[2], (D // 16) ** (-0.5)
    )
    expand_out = adam_update(expand_master, expand_first, expand_second, gradients[3], D ** (-0.5))
    expand_bias_out = adam_update(
        expand_bias_master, expand_bias_first, expand_bias_second, gradients[4], 0.5
    )
    shrink_out = adam_update(shrink_master, shrink_first, shrink_second, gradients[5], FF ** (-0.5))
    vector_out = adam_update(vector_master, vector_first, vector_second, vector_reduced, 0.3)
    block_output = jnp.concatenate(outputs, axis=0)
    input_grad = jnp.concatenate(input_grads, axis=0)
    return (
        (block_output, input_grad)
        + triple_out
        + query_value_out
        + output_out
        + expand_out
        + expand_bias_out
        + shrink_out
        + vector_out
    )


def solution(mesh):
    placed = (
        P(("dp", "mp"), None, None),
        P(("dp", "mp"), None, None),
        P("dp", None),
        P(None, None, "mp"),
        P(None, "mp", None),
        P("mp", None),
        P(None, "mp"),
        P("mp", None),
        P("mp", None),
        P(),
        P(None, "dp", "mp"),
        P(None, "dp", "mp"),
        P(None, "dp", "mp"),
        P(None, "mp", "dp"),
        P(None, "mp", "dp"),
        P(None, "mp", "dp"),
        P("mp", "dp"),
        P("mp", "dp"),
        P("mp", "dp"),
        P("dp", "mp"),
        P("dp", "mp"),
        P("dp", "mp"),
        P("mp", "dp"),
        P("mp", "dp"),
        P("mp", "dp"),
        P("mp", "dp"),
        P("mp", "dp"),
        P("mp", "dp"),
        P(None, ("dp", "mp")),
        P(None, ("dp", "mp")),
        P(None, ("dp", "mp")),
    )
    return jax.shard_map(
        per_device,
        mesh=mesh,
        in_specs=placed,
        out_specs=(
            P(("dp", "mp"), None, None),
            P(("dp", "mp"), None, None),
            P(None, "dp", "mp"),
            P(None, "dp", "mp"),
            P(None, "dp", "mp"),
            P(None, "dp", "mp"),
            P(None, "mp", "dp"),
            P(None, "mp", "dp"),
            P(None, "mp", "dp"),
            P(None, "mp", "dp"),
            P("mp", "dp"),
            P("mp", "dp"),
            P("mp", "dp"),
            P("mp", "dp"),
            P("dp", "mp"),
            P("dp", "mp"),
            P("dp", "mp"),
            P("dp", "mp"),
            P("mp", "dp"),
            P("mp", "dp"),
            P("mp", "dp"),
            P("mp", "dp"),
            P("mp", "dp"),
            P("mp", "dp"),
            P("mp", "dp"),
            P("mp", "dp"),
            P(None, ("dp", "mp")),
            P(None, ("dp", "mp")),
            P(None, ("dp", "mp")),
            P(None, ("dp", "mp")),
        ),
        check_vma=False,
    )
```

profile of v0, /device:TPU:0, one launch (start us, length us, event | category | flops | bytes accessed | tf_op | source)
XLA Modules:
  0.0 1532.0 jit_solution(792180418235632875)
XLA Ops:
  12.9 40.4 %all-gather.17.cloned.1.call-done = bf16[4,288,768]{2,1,0:T(8,128)(2,1)} async-done(((bf16[1,288,768]{2,1,0:T(8,128)(2,1)}), bf16[4,288,768]{2,1,0:T(8,128)(2,1)}) %all-gather.17.cloned.1.call-update) | async-done | bytes 1769488 | tf_op jit(solution)/shard_map/all_gather | solution.py:163
  64.1 30.5 %all-gather.21.cloned.1.call-done = bf16[4,288,768]{2,1,0:T(8,128)(2,1)} async-done(((bf16[1,288,768]{2,1,0:T(8,128)(2,1)}), bf16[4,288,768]{2,1,0:T(8,128)(2,1)}) %all-gather.21.cloned.1.call-update) | async-done | bytes 1769488 | tf_op jit(solution)/shard_map/all_gather | solution.py:163
  105.7 29.8 %all-gather.29.cloned.1.call-done = bf16[4,288,768]{2,1,0:T(8,128)(2,1)} async-done(((bf16[1,288,768]{2,1,0:T(8,128)(2,1)}), bf16[4,288,768]{2,1,0:T(8,128)(2,1)}) %all-gather.29.cloned.1.call-update) | async-done | bytes 1769488 | tf_op jit(solution)/shard_map/all_gather | solution.py:163
  177.3 38.5 %reduce-scatter.32.cloned.1.call-done = bf16[1,288,768]{2,1,0:T(8,128)(2,1)} async-done(((bf16[4,288,768]{2,1,0:T(8,128)(2,1)}), bf16[1,288,768]{2,1,0:T(8,128)(2,1)}) %reduce-scatter.32.cloned.1.call-update) | async-done | bytes 442384 | tf_op jit(solution)/shard_map/reduce_scatter | solution.py:171
  215.9 39.7 %reduce-scatter.40.cloned.1.call-done = bf16[1,288,768]{2,1,0:T(8,128)(2,1)} async-done(((bf16[4,288,768]{2,1,0:T(8,128)(2,1)}), bf16[1,288,768]{2,1,0:T(8,128)(2,1)}) %reduce-scatter.40.cloned.1.call-update) | async-done | bytes 442384 | tf_op jit(solution)/shard_map/reduce_scatter | solution.py:171
  263.9 37.4 %all-gather.23.cloned.1.call-done = bf16[4,288,768]{2,1,0:T(8,128)(2,1)} async-done(((bf16[1,288,768]{2,1,0:T(8,128)(2,1)}), bf16[4,288,768]{2,1,0:T(8,128)(2,1)}) %all-gather.23.cloned.1.call-update) | async-done | bytes 1769488 | tf_op jit(solution)/shard_map/all_gather | solution.py:182
  306.1 36.6 %all-gather.19.cloned.1.call-done = bf16[4,288,768]{2,1,0:T(8,128)(2,1)} async-done(((bf16[1,288,768]{2,1,0:T(8,128)(2,1)}), bf16[4,288,768]{2,1,0:T(8,128)(2,1)}) %all-gather.19.cloned.1.call-update) | async-done | bytes 1769488 | tf_op jit(solution)/shard_map/all_gather | solution.py:182
  359.6 31.1 %reduce-scatter.30.cloned.1.call-done = bf16[1,288,768]{2,1,0:T(8,128)(2,1)} async-done(((bf16[4,288,768]{2,1,0:T(8,128)(2,1)}), bf16[1,288,768]{2,1,0:T(8,128)(2,1)}) %reduce-scatter.30.cloned.1.call-update) | async-done | bytes 442384 | tf_op jit(solution)/shard_map/reduce_scatter | solution.py:188
  390.7 39.7 %reduce-scatter.34.cloned.1.call-done = bf16[1,288,768]{2,1,0:T(8,128)(2,1)} async-done(((bf16[4,288,768]{2,1,0:T(8,128)(2,1)}), bf16[1,288,768]{2,1,0:T(8,128)(2,1)}) %reduce-scatter.34.cloned.1.call-update) | async-done | bytes 442384 | tf_op jit(solution)/shard_map/reduce_scatter | solution.py:188
  434.8 39.5 %all-gather.31.cloned.1.call-done = bf16[4,288,768]{2,1,0:T(8,128)(2,1)} async-done(((bf16[1,288,768]{2,1,0:T(8,128)(2,1)}), bf16[4,288,768]{2,1,0:T(8,128)(2,1)}) %all-gather.31.cloned.1.call-update) | async-done | bytes 1769488 | tf_op jit(solution)/shard_map/all_gather | solution.py:182
  489.9 31.0 %reduce-scatter.42.cloned.1.call-done = bf16[1,288,768]{2,1,0:T(8,128)(2,1)} async-done(((bf16[4,288,768]{2,1,0:T(8,128)(2,1)}), bf16[1,288,768]{2,1,0:T(8,128)(2,1)}) %reduce-scatter.42.cloned.1.call-update) | async-done | bytes 442384 | tf_op jit(solution)/shard_map/reduce_scatter | solution.py:188
  612.6 30.6 %all-gather.45.cloned.1.call-done = bf16[4,288,768]{2,1,0:T(8,128)(2,1)} async-done(((bf16[1,288,768]{2,1,0:T(8,128)(2,1)}), bf16[4,288,768]{2,1,0:T(8,128)(2,1)}) %all-gather.45.cloned.1.call-update) | async-done | bytes 1769488 | tf_op jit(solution)/shard_map/all_gather | solution.py:201
  682.7 39.8 %reduce-scatter.48.cloned.1.call-done = bf16[1,288,768]{2,1,0:T(8,128)(2,1)} async-done(((bf16[4,288,768]{2,1,0:T(8,128)(2,1)}), bf16[1,288,768]{2,1,0:T(8,128)(2,1)}) %reduce-scatter.48.cloned.1.call-update) | async-done | bytes 442384 | tf_op jit(solution)/shard_map/reduce_scatter | solution.py:206
  722.6 40.3 %reduce-scatter.56.cloned.1.call-done = bf16[1,288,768]{2,1,0:T(8,128)(2,1)} async-done(((bf16[4,288,768]{2,1,0:T(8,128)(2,1)}), bf16[1,288,768]{2,1,0:T(8,128)(2,1)}) %reduce-scatter.56.cloned.1.call-update) | async-done | bytes 442384 | tf_op jit(solution)/shard_map/reduce_scatter | solution.py:206
  769.1 39.5 %all-gather.27.cloned.1.call-done = bf16[4,288,768]{2,1,0:T(8,128)(2,1)} async-done(((bf16[1,288,768]{2,1,0:T(8,128)(2,1)}), bf16[4,288,768]{2,1,0:T(8,128)(2,1)}) %all-gather.27.cloned.1.call-update) | async-done | bytes 1769488 | tf_op jit(solution)/shard_map/all_gather | solution.py:182
  818.9 36.2 %reduce-scatter.38.cloned.1.call-done = bf16[1,288,768]{2,1,0:T(8,128)(2,1)} async-done(((bf16[4,288,768]{2,1,0:T(8,128)(2,1)}), bf16[1,288,768]{2,1,0:T(8,128)(2,1)}) %reduce-scatter.38.cloned.1.call-update) | async-done | bytes 442384 | tf_op jit(solution)/shard_map/reduce_scatter | solution.py:188
  860.2 36.0 %all-gather.33.cloned.1.call-done = bf16[4,288,768]{2,1,0:T(8,128)(2,1)} async-done(((bf16[1,288,768]{2,1,0:T(8,128)(2,1)}), bf16[4,288,768]{2,1,0:T(8,128)(2,1)}) %all-gather.33.cloned.1.call-update) | async-done | bytes 1769488 | tf_op jit(solution)/shard_map/all_gather | solution.py:201
  906.3 30.7 %all-gather.41.cloned.1.call-done = bf16[4,288,768]{2,1,0:T(8,128)(2,1)} async-done(((bf16[1,288,768]{2,1,0:T(8,128)(2,1)}), bf16[4,288,768]{2,1,0:T(8,128)(2,1)}) %all-gather.41.cloned.1.call-update) | async-done | bytes 1769488 | tf_op jit(solution)/shard_map/all_gather | solution.py:201
  976.6 40.4 %reduce-scatter.52.cloned.1.call-done = bf16[1,288,768]{2,1,0:T(8,128)(2,1)} async-done(((bf16[4,288,768]{2,1,0:T(8,128)(2,1)}), bf16[1,288,768]{2,1,0:T(8,128)(2,1)}) %reduce-scatter.52.cloned.1.call-update) | async-done | bytes 442384 | tf_op jit(solution)/shard_map/reduce_scatter | solution.py:206
  1152.6 34.1 %all-gather.47.cloned.1.call-done = bf16[4,288,768]{2,1,0:T(8,128)(2,1)} async-done(((bf16[1,288,768]{2,1,0:T(8,128)(2,1)}), bf16[4,288,768]{2,1,0:T(8,128)(2,1)}) %all-gather.47.cloned.1.call-update) | async-done | bytes 1769488 | tf_op jit(solution)/shard_map/all_gather | solution.py:217
  1290.6 39.5 %all-reduce.2 = f32[6,768]{1,0:T(8,128)S(1)} all-reduce(f32[6,768]{1,0:T(8,128)S(1)} %add_add_fusion.8), channel_id=24, replica_groups=mesh['dp'=8,'mp'=4] {'dp','mp'}, use_global_device_ids=true, to_apply=%region_98.99.clone | all-reduce | flops 4608 | bytes 36864
  1402.3 37.8 %reduce-scatter.54.cloned.1.call-done = bf16[1,288,768]{2,1,0:T(8,128)(2,1)} async-done(((bf16[4,288,768]{2,1,0:T(8,128)(2,1)}), bf16[1,288,768]{2,1,0:T(8,128)(2,1)}) %reduce-scatter.54.cloned.1.call-update) | async-done | bytes 442384 | tf_op jit(solution)/shard_map/reduce_scatter | solution.py:222
  1442.2 38.5 %reduce-scatter.58.cloned.1.call-done = bf16[1,288,768]{2,1,0:T(8,128)(2,1)} async-done(((bf16[4,288,768]{2,1,0:T(8,128)(2,1)}), bf16[1,288,768]{2,1,0:T(8,128)(2,1)}) %reduce-scatter.58.cloned.1.call-update) | async-done | bytes 442384 | tf_op jit(solution)/shard_map/reduce_scatter | solution.py:222
  1482.7 37.7 %reduce-scatter.46.cloned.1.call-done = bf16[1,288,768]{2,1,0:T(8,128)(2,1)} async-done(((bf16[4,288,768]{2,1,0:T(8,128)(2,1)}), bf16[1,288,768]{2,1,0:T(8,128)(2,1)}) %reduce-scatter.46.cloned.1.call-update) | async-done | bytes 442384 | tf_op jit(solution)/shard_map/reduce_scatter | solution.py:222
  (714 shorter events, 638.8 us)
Async XLA Ops:
  10.8 124.6 %all-gather.29.cloned.1.call-start = ((), (), s32[]{:S(2)}) async-start(), calls=%async_computation.32 | async-start | bytes 2211840 | tf_op jit(solution)/shard_map/all_gather | solution.py:163
  11.5 163.9 %reduce-scatter.28.cloned.1.call-start = ((), (), s32[]{:S(2)}) async-start(), calls=%async_computation.21 | async-start | bytes 2211840 | tf_op jit(solution)/shard_map/reduce_scatter | solution.py:171
  63.8 152.1 %reduce-scatter.32.cloned.1.call-start = ((), (), s32[]{:S(2)}) async-start(), calls=%async_computation.25 | async-start | bytes 2211840 | tf_op jit(solution)/shard_map/reduce_scatter | solution.py:171
  105.1 150.5 %reduce-scatter.40.cloned.1.call-start = ((), (), s32[]{:S(2)}) async-start(), calls=%async_computation.33 | async-start | bytes 2211840 | tf_op jit(solution)/shard_map/reduce_scatter | solution.py:171
  146.0 155.3 %all-gather.23.cloned.1.call-start = ((), (), s32[]{:S(2)}) async-start(), calls=%async_computation.26 | async-start | bytes 2211840 | tf_op jit(solution)/shard_map/all_gather | solution.py:182
  262.5 128.2 %reduce-scatter.30.cloned.1.call-start = ((), (), s32[]{:S(2)}) async-start(), calls=%async_computation.23 | async-start | bytes 2211840 | tf_op jit(solution)/shard_map/reduce_scatter | solution.py:188
  484.3 118.3 %all-gather.37.cloned.1.call-start = ((), (), s32[]{:S(2)}) async-start(), calls=%async_computation.40 | async-start | bytes 2211840 | tf_op jit(solution)/shard_map/all_gather | solution.py:201
  530.4 152.3 %reduce-scatter.36.cloned.1.call-start = ((), (), s32[]{:S(2)}) async-start(), calls=%async_computation.29 | async-start | bytes 2211840 | tf_op jit(solution)/shard_map/reduce_scatter | solution.py:171
  572.8 149.7 %reduce-scatter.48.cloned.1.call-start = ((), (), s32[]{:S(2)}) async-start(), calls=%async_computation.41 | async-start | bytes 2211840 | tf_op jit(solution)/shard_map/reduce_scatter | solution.py:206
  612.6 150.2 %reduce-scatter.56.cloned.1.call-start = ((), (), s32[]{:S(2)}) async-start(), calls=%async_computation.49 | async-start | bytes 2211840 | tf_op jit(solution)/shard_map/reduce_scatter | solution.py:206
  653.3 155.3 %all-gather.27.cloned.1.call-start = ((), (), s32[]{:S(2)}) async-start(), calls=%async_computation.30 | async-start | bytes 2211840 | tf_op jit(solution)/shard_map/all_gather | solution.py:182
  818.4 118.5 %all-gather.41.cloned.1.call-start = ((), (), s32[]{:S(2)}) async-start(), calls=%async_computation.44 | async-start | bytes 2211840 | tf_op jit(solution)/shard_map/all_gather | solution.py:201
  860.1 116.5 %reduce-scatter.44.cloned.1.call-start = ((), (), s32[]{:S(2)}) async-start(), calls=%async_computation.37 | async-start | bytes 2211840 | tf_op jit(solution)/shard_map/reduce_scatter | solution.py:206
  947.0 117.7 %all-gather.39.cloned.1.call-start = ((), (), s32[]{:S(2)}) async-start(), calls=%async_computation.42 | async-start | bytes 2211840 | tf_op jit(solution)/shard_map/all_gather | solution.py:217
  1027.1 118.8 %all-gather.35.cloned.1.call-start = ((), (), s32[]{:S(2)}) async-start(), calls=%async_computation.38 | async-start | bytes 2211840 | tf_op jit(solution)/shard_map/all_gather | solution.py:217
  1033.2 153.6 %all-gather.47.cloned.1.call-start = ((), (), s32[]{:S(2)}) async-start(), calls=%async_computation.50 | async-start | bytes 2211840 | tf_op jit(solution)/shard_map/all_gather | solution.py:217
  1034.1 301.2 %reduce-scatter.60.cloned.1.call-start = ((), (), s32[]{:S(2)}) async-start(), calls=%async_computation.52 | async-start | bytes 2654208 | tf_op jit(solution)/shard_map/reduce_scatter | solution.py:269
  1045.6 292.9 %reduce-scatter.62.cloned.1.call-start = ((), (), s32[]{:S(2)}) async-start(), calls=%async_computation.53 | async-start | bytes 2654208 | tf_op jit(solution)/shard_map/reduce_scatter | solution.py:271
  1057.8 313.6 %reduce-scatter.66.cloned.1.call-start = ((), (), s32[]{:S(2)}) async-start(), calls=%async_computation.55 | async-start | bytes 884736
  1246.6 126.6 %reduce-scatter.64.cloned.1.call-start = ((), (), s32[]{:S(2)}) async-start(), calls=%async_computation.54 | async-start | bytes 2211840
  1266.2 134.2 %reduce-scatter.50.cloned.1.call-start = ((), (), s32[]{:S(2)}) async-start(), calls=%async_computation.43 | async-start | bytes 2211840 | tf_op jit(solution)/shard_map/reduce_scatter | solution.py:222
  1270.9 169.3 %reduce-scatter.54.cloned.1.call-start = ((), (), s32[]{:S(2)}) async-start(), calls=%async_computation.47 | async-start | bytes 2211840 | tf_op jit(solution)/shard_map/reduce_scatter | solution.py:222
  1275.4 205.3 %reduce-scatter.58.cloned.1.call-start = ((), (), s32[]{:S(2)}) async-start(), calls=%async_computation.51 | async-start | bytes 2211840 | tf_op jit(solution)/shard_map/reduce_scatter | solution.py:222
  1280.3 240.1 %reduce-scatter.46.cloned.1.call-start = ((), (), s32[]{:S(2)}) async-start(), calls=%async_computation.39 | async-start | bytes 2211840 | tf_op jit(solution)/shard_map/reduce_scatter | solution.py:222
  (202 other events, 3090.3 us)
Sparse Core Ops, SparseCore 0:
  10.2 43.0 all-gather.16
  55.4 39.1 all-gather.20
  96.2 39.1 all-gather.28
  218.0 37.4 reduce-scatter.39
  261.8 39.4 all-gather.22
  303.5 39.1 all-gather.18
  434.8 39.4 all-gather.30
  522.5 39.4 all-gather.24
  563.4 39.1 all-gather.36
  604.0 39.1 all-gather.44
  685.0 37.4 reduce-scatter.47
  769.1 39.4 all-gather.26
  856.7 39.4 all-gather.32
  897.7 39.1 all-gather.40
  1025.2 39.4 all-gather.38
  1066.1 39.1 all-gather.42
  1106.7 39.1 all-gather.34
  1147.5 39.1 all-gather.46
  1190.1 41.3 reduce-scatter.59
  1235.1 42.4 reduce-scatter.61
  1319.3 40.3 reduce-scatter.63
  1361.9 38.3 reduce-scatter.49
  1402.7 37.4 reduce-scatter.53
  1482.9 37.4 reduce-scatter.45
  (12 shorter events, 445.4 us)
where the time goes:
time: 1540 us; the launch traced here: 1530 us
  waiting for transfers between devices  1060 us (69%)
  matrix products  212 us (14%)
  other arithmetic  88 us (6%)
  local copies, waits for them, and re-layouts  85.2 us (6%)
  blocking collectives  62.8 us (4%)
  between operations  17.8 us (1%)
    all_gather x4, waiting for transfers between devices, per_device(): full_hidden = lax.all_gather(hidden_low, 'mp', axis=0, tiled=True)  153 us
    reduce_scatter x4, waiting for transfers between devices, per_device(): lax.psum_scatter(jnp.einsum('rlf,df->rld', dexpanded, expand_local, prefe...  149 us
    reduce_scatter x4, waiting for transfers between devices, per_device(): lax.psum_scatter(jnp.einsum('rlf,fd->rld', active, shrink_local, preferre...  138 us
    reduce_scatter x4, waiting for transfers between devices, per_device(): lax.psum_scatter(jnp.einsum('rle,ed->rld', context, output_local, preferr...  136 us
    reduce_scatter x4, waiting for transfers between devices, per_device(): lax.psum_scatter(jnp.einsum('rlje,jde->rld', dprojected, triple_local, pr...  133 us
    all_gather x4, waiting for transfers between devices, per_device(): full_inputs = lax.all_gather(own_inputs, 'mp', axis=0, tiled=True)  130 us
    all_gather x4, waiting for transfers between devices, per_device(): full_dsummed = lax.all_gather(dsummed_low, 'mp', axis=0, tiled=True)  127 us
    all_gather x4, waiting for transfers between devices, per_device(): full_dmixed = lax.all_gather(dmixed_low, 'mp', axis=0, tiled=True)  90.7 us
  transfers between devices with their start and end apart: 36, of which 32 were waited for; matrix products, arithmetic and copies ran while one was open for 19% of the time, Pallas kernels for 0%

commit v1 on v0

--- a/solution.py
+++ b/solution.py
@@ -160,7 +160,14 @@
         own_back = cotangent[micro_index * micro_rows : (micro_index + 1) * micro_rows].astype(
             jnp.float32
         )
-        full_inputs = lax.all_gather(own_inputs, "mp", axis=0, tiled=True)
+        ring = [own_inputs]
+        for hop in range(3):
+            ring.append(lax.ppermute(ring[-1], "mp", [(dev, (dev + 1) % 4) for dev in range(4)]))
+        full_inputs = jnp.roll(
+            jnp.concatenate(ring[::-1], axis=0),
+            (lax.axis_index("mp") + 1) * ring[0].shape[0],
+            axis=0,
+        )
         seg_rows = segment_blocks[:, micro_index].reshape(-1, length)
         allowed = seg_rows[:, :, None] == seg_rows[:, None, :]
         projected = jnp.einsum(

time: 1540 us -> 1480 us (0.961)
  waiting for transfers between devices: 1060 us -> 977 us
  starting transfers between devices: 3.51 us -> 20.3 us
    ppermute x0 -> x12, waiting for transfers between devices: none -> 146 us  [per_device(): lax.ppermute(ring[-1], 'mp', [(dev, (dev + 1) % 4) for dev in range(4)])]
    all_gather x4 -> x0, waiting for transfers between devices: 130 us -> none  [per_device(): full_inputs = lax.all_gather(own_inputs, 'mp', axis=0, tiled=True)]
    all_gather x4, waiting for transfers between devices: 127 us -> 76.2 us  [per_device(): full_dsummed = lax.all_gather(dsummed_low, 'mp', axis=0, tiled=True)]
    reduce_scatter x4, waiting for transfers between devices: 136 us -> 88.6 us  [per_device(): lax.psum_scatter(jnp.einsum('rle,ed->rld', context, output_local, preferr...]
    ppermute x0 -> x12, starting transfers between devices: none -> 16.8 us  [per_device(): lax.ppermute(ring[-1], 'mp', [(dev, (dev + 1) % 4) for dev in range(4)])]
    unnamed x403 -> x421, local copies, waits for them, and re-layouts: 59.1 us -> 60.3 us
  transfers between devices with their start and end apart: 36 -> 44, of which waited for: 32 -> 37; matrix products, arithmetic and copies ran while one was open for 19% -> 20% of each run, Pallas kernels for 0% -> 0%
where the time goes in v1:
time: 1480 us; the launch traced here: 1470 us
  waiting for transfers between devices  977 us (66%)
  matrix products  206 us (14%)
  other arithmetic  101 us (7%)
  local copies, waits for them, and re-layouts  86 us (6%)
  blocking collectives  62.8 us (4%)
  starting transfers between devices  20.3 us (1%)
  between operations  18 us (1%)
    all_gather x4, waiting for transfers between devices, per_device(): full_hidden = lax.all_gather(hidden_low, 'mp', axis=0, tiled=True)  153 us
    reduce_scatter x4, waiting for transfers between devices, per_device(): lax.psum_scatter(jnp.einsum('rlf,df->rld', dexpanded, expand_local, prefe...  150 us
    ppermute x12, waiting for transfers between devices, per_device(): lax.ppermute(ring[-1], 'mp', [(dev, (dev + 1) % 4) for dev in range(4)])  146 us
    reduce_scatter x4, waiting for transfers between devices, per_device(): lax.psum_scatter(jnp.einsum('rlf,fd->rld', active, shrink_local, preferre...  138 us
    reduce_scatter x4, waiting for transfers between devices, per_device(): lax.psum_scatter(jnp.einsum('rlje,jde->rld', dprojected, triple_local, pr...  133 us
    all_gather x4, waiting for transfers between devices, per_device(): full_dmixed = lax.all_gather(dmixed_low, 'mp', axis=0, tiled=True)  90.8 us
    reduce_scatter x4, waiting for transfers between devices, per_device(): lax.psum_scatter(jnp.einsum('rle,ed->rld', context, output_local, preferr...  88.6 us
    all_gather x4, waiting for transfers between devices, per_device(): full_dsummed = lax.all_gather(dsummed_low, 'mp', axis=0, tiled=True)  76.2 us
  transfers between devices with their start and end apart: 44, of which 37 were waited for; matrix products, arithmetic and copies ran while one was open for 20% of the time, Pallas kernels for 0%

profile of v1, /device:TPU:0, one launch (start us, length us, event | category | flops | bytes accessed | tf_op | source)
XLA Modules:
  0.0 1471.4 jit_solution(12612556283611229092)
XLA Ops:
  173.7 39.9 %reduce-scatter.40.cloned.1.call-done = bf16[1,288,768]{2,1,0:T(8,128)(2,1)} async-done(((bf16[4,288,768]{2,1,0:T(8,128)(2,1)}), bf16[1,288,768]{2,1,0:T(8,128)(2,1)}) %reduce-scatter.40.cloned.1.call-update) | async-done | bytes 442384 | tf_op jit(solution)/shard_map/reduce_scatter | solution.py:178
  221.7 37.6 %all-gather.15.cloned.1.call-done = bf16[4,288,768]{2,1,0:T(8,128)(2,1)} async-done(((bf16[1,288,768]{2,1,0:T(8,128)(2,1)}), bf16[4,288,768]{2,1,0:T(8,128)(2,1)}) %all-gather.15.cloned.1.call-update) | async-done | bytes 1769488 | tf_op jit(solution)/shard_map/all_gather | solution.py:189
  264.1 36.5 %all-gather.13.cloned.1.call-done = bf16[4,288,768]{2,1,0:T(8,128)(2,1)} async-done(((bf16[1,288,768]{2,1,0:T(8,128)(2,1)}), bf16[4,288,768]{2,1,0:T(8,128)(2,1)}) %all-gather.13.cloned.1.call-update) | async-done | bytes 1769488 | tf_op jit(solution)/shard_map/all_gather | solution.py:189
  317.6 30.9 %reduce-scatter.30.cloned.1.call-done = bf16[1,288,768]{2,1,0:T(8,128)(2,1)} async-done(((bf16[4,288,768]{2,1,0:T(8,128)(2,1)}), bf16[1,288,768]{2,1,0:T(8,128)(2,1)}) %reduce-scatter.30.cloned.1.call-update) | async-done | bytes 442384 | tf_op jit(solution)/shard_map/reduce_scatter | solution.py:195
  348.5 39.8 %reduce-scatter.34.cloned.1.call-done = bf16[1,288,768]{2,1,0:T(8,128)(2,1)} async-done(((bf16[4,288,768]{2,1,0:T(8,128)(2,1)}), bf16[1,288,768]{2,1,0:T(8,128)(2,1)}) %reduce-scatter.34.cloned.1.call-update) | async-done | bytes 442384 | tf_op jit(solution)/shard_map/reduce_scatter | solution.py:195
  392.7 39.5 %all-gather.19.cloned.1.call-done = bf16[4,288,768]{2,1,0:T(8,128)(2,1)} async-done(((bf16[1,288,768]{2,1,0:T(8,128)(2,1)}), bf16[4,288,768]{2,1,0:T(8,128)(2,1)}) %all-gather.19.cloned.1.call-update) | async-done | bytes 1769488 | tf_op jit(solution)/shard_map/all_gather | solution.py:189
  448.2 30.7 %reduce-scatter.42.cloned.1.call-done = bf16[1,288,768]{2,1,0:T(8,128)(2,1)} async-done(((bf16[4,288,768]{2,1,0:T(8,128)(2,1)}), bf16[1,288,768]{2,1,0:T(8,128)(2,1)}) %reduce-scatter.42.cloned.1.call-update) | async-done | bytes 442384 | tf_op jit(solution)/shard_map/reduce_scatter | solution.py:195
  592.8 29.4 %reduce-scatter.36.cloned.1.call-done = bf16[1,288,768]{2,1,0:T(8,128)(2,1)} async-done(((bf16[4,288,768]{2,1,0:T(8,128)(2,1)}), bf16[1,288,768]{2,1,0:T(8,128)(2,1)}) %reduce-scatter.36.cloned.1.call-update) | async-done | bytes 442384 | tf_op jit(solution)/shard_map/reduce_scatter | solution.py:178
  622.2 40.0 %reduce-scatter.48.cloned.1.call-done = bf16[1,288,768]{2,1,0:T(8,128)(2,1)} async-done(((bf16[4,288,768]{2,1,0:T(8,128)(2,1)}), bf16[1,288,768]{2,1,0:T(8,128)(2,1)}) %reduce-scatter.48.cloned.1.call-update) | async-done | bytes 442384 | tf_op jit(solution)/shard_map/reduce_scatter | solution.py:213
  662.1 40.3 %reduce-scatter.56.cloned.1.call-done = bf16[1,288,768]{2,1,0:T(8,128)(2,1)} async-done(((bf16[4,288,768]{2,1,0:T(8,128)(2,1)}), bf16[1,288,768]{2,1,0:T(8,128)(2,1)}) %reduce-scatter.56.cloned.1.call-update) | async-done | bytes 442384 | tf_op jit(solution)/shard_map/reduce_scatter | solution.py:213
  708.7 39.5 %all-gather.17.cloned.1.call-done = bf16[4,288,768]{2,1,0:T(8,128)(2,1)} async-done(((bf16[1,288,768]{2,1,0:T(8,128)(2,1)}), bf16[4,288,768]{2,1,0:T(8,128)(2,1)}) %all-gather.17.cloned.1.call-update) | async-done | bytes 1769488 | tf_op jit(solution)/shard_map/all_gather | solution.py:189
  757.9 36.8 %reduce-scatter.38.cloned.1.call-done = bf16[1,288,768]{2,1,0:T(8,128)(2,1)} async-done(((bf16[4,288,768]{2,1,0:T(8,128)(2,1)}), bf16[1,288,768]{2,1,0:T(8,128)(2,1)}) %reduce-scatter.38.cloned.1.call-update) | async-done | bytes 442384 | tf_op jit(solution)/shard_map/reduce_scatter | solution.py:195
  800.2 35.4 %all-gather.21.cloned.1.call-done = bf16[4,288,768]{2,1,0:T(8,128)(2,1)} async-done(((bf16[1,288,768]{2,1,0:T(8,128)(2,1)}), bf16[4,288,768]{2,1,0:T(8,128)(2,1)}) %all-gather.21.cloned.1.call-update) | async-done | bytes 1769488 | tf_op jit(solution)/shard_map/all_gather | solution.py:208
  845.7 30.5 %all-gather.29.cloned.1.call-done = bf16[4,288,768]{2,1,0:T(8,128)(2,1)} async-done(((bf16[1,288,768]{2,1,0:T(8,128)(2,1)}), bf16[4,288,768]{2,1,0:T(8,128)(2,1)}) %all-gather.29.cloned.1.call-update) | async-done | bytes 1769488 | tf_op jit(solution)/shard_map/all_gather | solution.py:208
  886.9 29.0 %reduce-scatter.44.cloned.1.call-done = bf16[1,288,768]{2,1,0:T(8,128)(2,1)} async-done(((bf16[4,288,768]{2,1,0:T(8,128)(2,1)}), bf16[1,288,768]{2,1,0:T(8,128)(2,1)}) %reduce-scatter.44.cloned.1.call-update) | async-done | bytes 442384 | tf_op jit(solution)/shard_map/reduce_scatter | solution.py:213
  915.9 40.4 %reduce-scatter.52.cloned.1.call-done = bf16[1,288,768]{2,1,0:T(8,128)(2,1)} async-done(((bf16[4,288,768]{2,1,0:T(8,128)(2,1)}), bf16[1,288,768]{2,1,0:T(8,128)(2,1)}) %reduce-scatter.52.cloned.1.call-update) | async-done | bytes 442384 | tf_op jit(solution)/shard_map/reduce_scatter | solution.py:213
  1019.5 25.2 %all-gather.31.cloned.1.call-done = bf16[4,288,768]{2,1,0:T(8,128)(2,1)} async-done(((bf16[1,288,768]{2,1,0:T(8,128)(2,1)}), bf16[4,288,768]{2,1,0:T(8,128)(2,1)}) %all-gather.31.cloned.1.call-update) | async-done | bytes 1769488 | tf_op jit(solution)/shard_map/all_gather | solution.py:224
  1060.3 25.2 %all-gather.23.cloned.1.call-done = bf16[4,288,768]{2,1,0:T(8,128)(2,1)} async-done(((bf16[1,288,768]{2,1,0:T(8,128)(2,1)}), bf16[4,288,768]{2,1,0:T(8,128)(2,1)}) %all-gather.23.cloned.1.call-update) | async-done | bytes 1769488 | tf_op jit(solution)/shard_map/all_gather | solution.py:224
  1092.1 34.0 %all-gather.35.cloned.1.call-done = bf16[4,288,768]{2,1,0:T(8,128)(2,1)} async-done(((bf16[1,288,768]{2,1,0:T(8,128)(2,1)}), bf16[4,288,768]{2,1,0:T(8,128)(2,1)}) %all-gather.35.cloned.1.call-update) | async-done | bytes 1769488 | tf_op jit(solution)/shard_map/all_gather | solution.py:224
  1230.0 39.4 %all-reduce.2 = f32[6,768]{1,0:T(8,128)S(1)} all-reduce(f32[6,768]{1,0:T(8,128)S(1)} %add_add_fusion.8), channel_id=24, replica_groups=mesh['dp'=8,'mp'=4] {'dp','mp'}, use_global_device_ids=true, to_apply=%region_98.100.clone | all-reduce | flops 4608 | bytes 36864
  1284.1 23.4 %all-reduce.3 = (f32[2,3,64]{2,1,0:T(4,128)S(1)}, f32[12,64]{1,0:T(8,128)S(1)}) all-reduce(f32[2,3,64]{2,1,0:T(4,128)S(1)} %reshape.574, f32[12,64]{1,0:T(8,128)S(1)} %add.691), channel_id=19, replica_groups=mesh['dp'=8,'mp'=4] {'dp'}, use_global_device_ids=true, to_apply=%region_65.67.clone | all-reduce | flops 1152 | bytes 9216
  1341.8 37.7 %reduce-scatter.54.cloned.1.call-done = bf16[1,288,768]{2,1,0:T(8,128)(2,1)} async-done(((bf16[4,288,768]{2,1,0:T(8,128)(2,1)}), bf16[1,288,768]{2,1,0:T(8,128)(2,1)}) %reduce-scatter.54.cloned.1.call-update) | async-done | bytes 442384 | tf_op jit(solution)/shard_map/reduce_scatter | solution.py:229
  1381.4 38.5 %reduce-scatter.58.cloned.1.call-done = bf16[1,288,768]{2,1,0:T(8,128)(2,1)} async-done(((bf16[4,288,768]{2,1,0:T(8,128)(2,1)}), bf16[1,288,768]{2,1,0:T(8,128)(2,1)}) %reduce-scatter.58.cloned.1.call-update) | async-done | bytes 442384 | tf_op jit(solution)/shard_map/reduce_scatter | solution.py:229
  1422.0 37.9 %reduce-scatter.46.cloned.1.call-done = bf16[1,288,768]{2,1,0:T(8,128)(2,1)} async-done(((bf16[4,288,768]{2,1,0:T(8,128)(2,1)}), bf16[1,288,768]{2,1,0:T(8,128)(2,1)}) %reduce-scatter.46.cloned.1.call-update) | async-done | bytes 442384 | tf_op jit(solution)/shard_map/reduce_scatter | solution.py:229
  (748 shorter events, 616.0 us)
Async XLA Ops:
  7.2 145.3 %reduce-scatter.28.cloned.1.call-start = ((), (), s32[]{:S(2)}) async-start(), calls=%async_computation.20 | async-start | bytes 2211840 | tf_op jit(solution)/shard_map/reduce_scatter | solution.py:178
  70.9 102.8 %reduce-scatter.32.cloned.1.call-start = ((), (), s32[]{:S(2)}) async-start(), calls=%async_computation.23 | async-start | bytes 2211840 | tf_op jit(solution)/shard_map/reduce_scatter | solution.py:178
  151.9 107.4 %all-gather.15.cloned.1.call-start = ((), (), s32[]{:S(2)}) async-start(), calls=%async_computation.24 | async-start | bytes 2211840 | tf_op jit(solution)/shard_map/all_gather | solution.py:189
  220.3 128.2 %reduce-scatter.30.cloned.1.call-start = ((), (), s32[]{:S(2)}) async-start(), calls=%async_computation.22 | async-start | bytes 2211840 | tf_op jit(solution)/shard_map/reduce_scatter | solution.py:195
  316.3 116.0 %all-gather.19.cloned.1.call-start = ((), (), s32[]{:S(2)}) async-start(), calls=%async_computation.30 | async-start | bytes 2211840 | tf_op jit(solution)/shard_map/all_gather | solution.py:189
  441.5 120.7 %all-gather.25.cloned.1.call-start = ((), (), s32[]{:S(2)}) async-start(), calls=%async_computation.36 | async-start | bytes 2211840 | tf_op jit(solution)/shard_map/all_gather | solution.py:208
  487.8 94.9 %all-gather.33.cloned.1.call-start = ((), (), s32[]{:S(2)}) async-start(), calls=%async_computation.44 | async-start | bytes 2211840 | tf_op jit(solution)/shard_map/all_gather | solution.py:208
  562.1 100.0 %reduce-scatter.48.cloned.1.call-start = ((), (), s32[]{:S(2)}) async-start(), calls=%async_computation.37 | async-start | bytes 2211840 | tf_op jit(solution)/shard_map/reduce_scatter | solution.py:213
  572.2 130.2 %reduce-scatter.56.cloned.1.call-start = ((), (), s32[]{:S(2)}) async-start(), calls=%async_computation.45 | async-start | bytes 2211840 | tf_op jit(solution)/shard_map/reduce_scatter | solution.py:213
  592.7 155.4 %all-gather.17.cloned.1.call-start = ((), (), s32[]{:S(2)}) async-start(), calls=%async_computation.27 | async-start | bytes 2211840 | tf_op jit(solution)/shard_map/all_gather | solution.py:189
  757.9 118.3 %all-gather.29.cloned.1.call-start = ((), (), s32[]{:S(2)}) async-start(), calls=%async_computation.40 | async-start | bytes 2211840 | tf_op jit(solution)/shard_map/all_gather | solution.py:208
  799.7 116.2 %reduce-scatter.44.cloned.1.call-start = ((), (), s32[]{:S(2)}) async-start(), calls=%async_computation.33 | async-start | bytes 2211840 | tf_op jit(solution)/shard_map/reduce_scatter | solution.py:213
  845.7 110.6 %reduce-scatter.52.cloned.1.call-start = ((), (), s32[]{:S(2)}) async-start(), calls=%async_computation.41 | async-start | bytes 2211840 | tf_op jit(solution)/shard_map/reduce_scatter | solution.py:213
  886.3 117.6 %all-gather.27.cloned.1.call-start = ((), (), s32[]{:S(2)}) async-start(), calls=%async_computation.38 | async-start | bytes 2211840 | tf_op jit(solution)/shard_map/all_gather | solution.py:224
  966.4 119.1 %all-gather.23.cloned.1.call-start = ((), (), s32[]{:S(2)}) async-start(), calls=%async_computation.34 | async-start | bytes 2211840 | tf_op jit(solution)/shard_map/all_gather | solution.py:224
  972.2 153.9 %all-gather.35.cloned.1.call-start = ((), (), s32[]{:S(2)}) async-start(), calls=%async_computation.46 | async-start | bytes 2211840 | tf_op jit(solution)/shard_map/all_gather | solution.py:224
  973.1 301.5 %reduce-scatter.60.cloned.1.call-start = ((), (), s32[]{:S(2)}) async-start(), calls=%async_computation.48 | async-start | bytes 2654208 | tf_op jit(solution)/shard_map/reduce_scatter | solution.py:276
  984.9 293.0 %reduce-scatter.62.cloned.1.call-start = ((), (), s32[]{:S(2)}) async-start(), calls=%async_computation.49 | async-start | bytes 2654208 | tf_op jit(solution)/shard_map/reduce_scatter | solution.py:278
  997.0 313.7 %reduce-scatter.66.cloned.1.call-start = ((), (), s32[]{:S(2)}) async-start(), calls=%async_computation.51 | async-start | bytes 884736
  1186.0 126.5 %reduce-scatter.64.cloned.1.call-start = ((), (), s32[]{:S(2)}) async-start(), calls=%async_computation.50 | async-start | bytes 2211840
  1205.5 134.2 %reduce-scatter.50.cloned.1.call-start = ((), (), s32[]{:S(2)}) async-start(), calls=%async_computation.39 | async-start | bytes 2211840 | tf_op jit(solution)/shard_map/reduce_scatter | solution.py:229
  1210.3 169.2 %reduce-scatter.54.cloned.1.call-start = ((), (), s32[]{:S(2)}) async-start(), calls=%async_computation.43 | async-start | bytes 2211840 | tf_op jit(solution)/shard_map/reduce_scatter | solution.py:229
  1214.8 205.2 %reduce-scatter.58.cloned.1.call-start = ((), (), s32[]{:S(2)}) async-start(), calls=%async_computation.47 | async-start | bytes 2211840 | tf_op jit(solution)/shard_map/reduce_scatter | solution.py:229
  1219.7 240.1 %reduce-scatter.46.cloned.1.call-start = ((), (), s32[]{:S(2)}) async-start(), calls=%async_computation.35 | async-start | bytes 2211840 | tf_op jit(solution)/shard_map/reduce_scatter | solution.py:229
  (219 other events, 2976.9 us)
Sparse Core Ops, SparseCore 0:
  71.0 62.9 reduce-scatter.27
  176.0 37.4 reduce-scatter.39
  219.8 39.4 all-gather.14
  261.3 39.1 all-gather.12
  350.8 37.4 reduce-scatter.33
  392.8 39.4 all-gather.18
  487.9 53.7 all-gather.24
  543.3 39.4 all-gather.32
  624.6 37.4 reduce-scatter.47
  664.9 37.4 reduce-scatter.55
  708.7 39.4 all-gather.16
  796.1 39.4 all-gather.20
  837.0 39.1 all-gather.28
  918.7 37.4 reduce-scatter.51
  964.5 39.4 all-gather.26
  1005.5 39.1 all-gather.30
  1046.3 39.1 all-gather.22
  1086.9 39.1 all-gather.34
  1129.5 41.3 reduce-scatter.59
  1174.5 42.4 reduce-scatter.61
  1258.5 40.3 reduce-scatter.63
  1301.3 38.3 reduce-scatter.49
  1341.9 37.4 reduce-scatter.53
  1382.4 37.4 reduce-scatter.57
  (8 shorter events, 295.0 us)
